TPU v7x, 512 devices: a whole 4x8x8 slice. The times are simulated.
512 devices in a mesh: rot: 32 (over y, x_hi, core), tag: 16 (over z, x_lo).
Axes of the slice: x: 4 (x_hi: 2, x_lo: 2; x = x_hi * 2 + x_lo), y: 8, z: 8, core: 2. Of those that a mesh axis runs over, the one named last changes fastest.
Arguments:
- user_factors: bfloat16 [262144, 512], P(('rot', 'tag')), may hold values from -1.1953125 to 1.1953125
- item_factors: bfloat16 [32768, 512], P('rot'), may hold values from -1.1953125 to 1.1953125
- tag_factors: bfloat16 [8192, 512], P('tag'), may hold values from -1.1953125 to 1.1953125
- rating_tiles: int32 [8192, 2], P(('rot', 'tag')), may hold values from 0 to 7, as said below
- rating_counts: int32 [512], P(('rot', 'tag')), may hold values from 1 to 16, as said below
- ratings: bfloat16 [8192, 128, 128], P(('rot', 'tag')), may hold values from -6 to 6
- tag_tiles: int32 [8192, 2], P(('rot', 'tag')), may hold values from 0 to 7, as said below
- tag_values: bfloat16 [8192, 128, 128], P(('rot', 'tag')), may hold values from -6 to 6
Outputs:
- new_users: bfloat16 [262144, 512], P(('rot', 'tag'))
- rotated_items: bfloat16 [32768, 512], P('rot')
- new_tags: bfloat16 [8192, 512], P('tag')
Inputs may be any that keep to these rules, and one draw needn't show every extreme that they name: `rating_tiles`: each device's 16 slots hold distinct tiles; column 0 is below 4, column 1 below 8. `rating_counts`: uneven over devices; some device has all 16 slots live. `tag_tiles`: each device has exactly 16 distinct tiles; column 0 is below 8, column 1 below 4.
All inputs are finite; a program needn't handle non-finite values.
Results may differ from a plain program's by a relative error of at most 0.0043.
Values may be sent and summed in bfloat16 or wider, within the bound.
No kernel may reach another device: no remote copies, remote signals or barrier semaphores. Data moves between devices by JAX's collectives and lax.ppermute only.
A program may use at most 64 MiB of HBM per device.

v0:
```python
import jax
import jax.numpy as jnp
from jax import lax
from jax.sharding import PartitionSpec as P

TILE = 128


def shifted(block, axis, distance):
    devices = range(lax.axis_size(axis))
    route = [((i - distance) % len(devices), i) for i in devices]
    return lax.ppermute(block, axis, route)


def spread_tiles(index, count, tiles):
    empty = jnp.zeros((count,) + tiles.shape[1:], jnp.float32)
    return empty.at[index].add(tiles)


def on_device(
    user_factors,
    item_factors,
    tag_factors,
    rating_tiles,
    rating_counts,
    ratings,
    tag_tiles,
    tag_values,
):
    user_count = user_factors.shape[0]
    item_count = item_factors.shape[0]
    tag_count = tag_factors.shape[0]
    rank = user_factors.shape[1]
    ublock = user_factors.reshape(user_count // TILE, TILE, rank)
    vblock = item_factors.reshape(item_count // TILE, TILE, rank)
    wblock = tag_factors.reshape(tag_count // TILE, TILE, rank)
    user_tiles = ublock[rating_tiles[:, 0]]
    item_tiles = vblock[rating_tiles[:, 1]]
    predicted = jnp.einsum(
        "sur,sir->sui", user_tiles, item_tiles, preferred_element_type=jnp.float32
    )
    live = (jnp.arange(rating_tiles.shape[0]) < rating_counts[0])[:, None, None]
    rating_err = jnp.where(live, predicted - ratings.astype(jnp.float32), 0.0).astype(jnp.bfloat16)
    user_part = jnp.einsum(
        "sui,sir->sur", rating_err, item_tiles, preferred_element_type=jnp.float32
    )
    item_part = jnp.einsum(
        "sui,sur->sir", rating_err, user_tiles, preferred_element_type=jnp.float32
    )
    item_rows = vblock[tag_tiles[:, 0]]
    tag_rows = wblock[tag_tiles[:, 1]]
    tag_err = (
        jnp.einsum("sir,sjr->sij", item_rows, tag_rows, preferred_element_type=jnp.float32)
        - tag_values.astype(jnp.float32)
    ).astype(jnp.bfloat16)
    item_from_tags = jnp.einsum(
        "sij,sjr->sir", tag_err, tag_rows, preferred_element_type=jnp.float32
    )
    tag_part = jnp.einsum("sij,sir->sjr", tag_err, item_rows, preferred_element_type=jnp.float32)
    user_grad = spread_tiles(rating_tiles[:, 0], user_count // TILE, user_part).reshape(
        user_count, rank
    )
    item_grad = spread_tiles(rating_tiles[:, 1], item_count // TILE, item_part)
    item_grad = item_grad.at[tag_tiles[:, 0]].add(item_from_tags).reshape(item_count, rank)
    tag_grad = spread_tiles(tag_tiles[:, 1], tag_count // TILE, tag_part).reshape(tag_count, rank)
    users32 = user_factors.astype(jnp.float32)
    new_users = (users32 - 0.04 * (user_grad + 0.05 * users32)).astype(jnp.bfloat16)
    total = lax.psum(item_grad, "tag")
    items32 = item_factors.astype(jnp.float32)
    new_items = (items32 - 0.04 * (total + 0.05 * items32)).astype(jnp.bfloat16)
    rotated_items = shifted(new_items, "rot", 1)
    tag_total = lax.psum(tag_grad, "rot")
    tags32 = tag_factors.astype(jnp.float32)
    new_tags = (tags32 - 0.04 * (tag_total + 0.05 * tags32)).astype(jnp.bfloat16)
    return (new_users, rotated_items, new_tags)


def solution(mesh):
    placed = (
        P(("rot", "tag"), None),
        P("rot", None),
        P("tag", None),
        P(("rot", "tag"), None),
        P(("rot", "tag")),
        P(("rot", "tag"), None, None),
        P(("rot", "tag"), None),
        P(("rot", "tag"), None, None),
    )
    return jax.shard_map(
        on_device,
        mesh=mesh,
        in_specs=placed,
        out_specs=(P(("rot", "tag"), None), P("rot", None), P("tag", None)),
        check_vma=False,
    )
```

profile of v0, /device:TPU:1, one launch (start us, length us, event | category | flops | bytes accessed | tf_op | source)
XLA Modules:
  0.0 487.4 jit_solution(15541563892529906015)
XLA Ops:
  7.2 0.0 all-reduce.3.cloned.1.call-start
  7.2 0.8 fusion.13
  8.6 0.0 copy-start.2
  8.7 3.2 gather_fusion
  11.8 0.0 copy-done.2
  11.8 0.7 gather_fusion.1
  12.5 0.0 copy-start.7
  12.5 0.0 copy-start.9
  12.5 3.2 fusion.4
  15.7 0.0 copy-done.7
  15.7 0.0 copy-done.9
  15.7 0.0 copy-start.11
  15.7 0.0 copy-start.13
  15.8 2.7 fusion.17
  18.5 0.0 copy-done.11
  18.5 0.0 copy-done.13
  18.5 0.7 gather_fusion.2
  19.2 0.0 copy-start.3
  19.2 3.4 gather_fusion.3
  22.6 0.0 copy-done.3
  22.6 2.5 fusion.5
  25.2 0.0 copy-start.10
  25.2 2.7 fusion.18
  27.9 0.2 broadcast_in_dim.16
  28.1 6.2 %scatter_fusion.1 = f32[8,128,512]{2,1,0:T(8,128)S(1)} fusion(f32[8,128,512]{2,1,0:T(8,128)S(1)} %broadcast_in_dim.16, s32[16]{0:T(128)S(1)} %get-tuple-element.5, f32[16,128,512]{2,1,0:T(8,128)} %fusion.17), kind=kCustom, calls=%fused_computation.5 | custom fusion | flops 1048576 | bytes 12582976 | tf_op jit(solution)/shard_map/scatter-add | solution.py:17
  34.3 6.2 %scatter_fusion.2 = f32[8,128,512]{2,1,0:T(8,128)S(1)} fusion(f32[8,128,512]{2,1,0:T(8,128)S(1)} %scatter_fusion.1, s32[16]{0:T(128)S(1)} %get-tuple-element.4, f32[16,128,512]{2,1,0:T(8,128)} %fusion.18), kind=kCustom, calls=%fused_computation.6 | custom fusion | flops 1048576 | bytes 12582976 | tf_op jit(solution)/shard_map/scatter-add | solution.py:64
  40.5 0.0 copy-start
  40.5 1.4 copy-done
  41.9 0.0 all-reduce.3.cloned.1.call-update
  41.9 0.0 all-reduce.5.cloned.1.call-start
  41.9 4.5 fusion.19
  46.4 0.1 broadcast.30.clone.1
  46.5 6.1 %scatter_fusion.3 = f32[4,128,512]{2,1,0:T(8,128)S(1)} fusion(f32[4,128,512]{2,1,0:T(8,128)S(1)} %broadcast.30.clone.1, s32[16]{0:T(128)S(1)} %get-tuple-element.3, f32[16,128,512]{2,1,0:T(8,128)} %fusion.19), kind=kCustom, calls=%fused_computation.7 | custom fusion | flops 1048576 | bytes 12582976 | tf_op jit(solution)/shard_map/scatter-add | solution.py:17
  52.6 1.0 copy-done.1
  53.6 0.0 all-reduce.5.cloned.1.call-update
  53.7 136.4 %all-reduce.3.cloned.1.call-done = f32[1024,512]{1,0:T(8,128)} async-done(((f32[1024,512]{1,0:T(8,128)}), f32[1024,512]{1,0:T(8,128)}) %all-reduce.3.cloned.1.call-update) | async-done | bytes 2097168 | tf_op jit(solution)/shard_map/psum | solution.py:68
  190.1 3.0 fusion.2
  193.1 14.7 %collective-permute-start = (bf16[1024,512]{1,0:T(8,128)(2,1)}, bf16[1024,512]{1,0:T(8,128)(2,1)}, u32[]{:S(2)}, u32[]{:S(2)}) collective-permute-start(bf16[1024,512]{1,0:T(8,128)(2,1)} %fusion.2), channel_id=1, source_target_pairs={{496,0},{0,16},{16,32},{32,48},{48,64},{64,80},{80,96},{96,112},{1... | collective-permute-start | bytes 3145736 | tf_op jit(solution)/shard_map/ppermute | solution.py:12
  207.8 2.6 fusion.16
  210.4 0.1 broadcast.30.clone
  210.5 0.0 copy-start.5
  210.6 6.1 %scatter_fusion = f32[4,128,512]{2,1,0:T(8,128)S(1)} fusion(f32[4,128,512]{2,1,0:T(8,128)S(1)} %broadcast.30.clone, s32[16]{0:T(128)S(1)} %get-tuple-element.6, f32[16,128,512]{2,1,0:T(8,128)} %fusion.16), kind=kCustom, calls=%fused_computation.4 | custom fusion | flops 1048576 | bytes 12582976 | tf_op jit(solution)/shard_map/scatter-add | solution.py:17
  216.7 0.0 copy-start.6
  216.7 1.0 fusion.8
  217.7 258.3 %all-reduce.5.cloned.1.call-done = f32[512,512]{1,0:T(8,128)} async-done(((f32[512,512]{1,0:T(8,128)}), f32[512,512]{1,0:T(8,128)}) %all-reduce.5.cloned.1.call-update) | async-done | bytes 1048592 | tf_op jit(solution)/shard_map/psum | solution.py:72
  476.0 2.2 fusion.11
  478.3 0.0 collective-permute-done
  478.3 2.3 copy.23
  (14 shorter events, 0.0 us)
Async XLA Ops:
  7.2 182.9 %all-reduce.3.cloned.1.call-start = ((), (), s32[]{:S(2)}) async-start(), calls=%async_computation | async-start | bytes 4194304 | tf_op jit(solution)/shard_map/psum | solution.py:68
  8.6 3.2 copy-start.2
  12.5 3.2 copy-start.7
  12.5 3.2 copy-start.9
  15.7 2.7 copy-start.11
  15.7 2.7 copy-start.13
  19.2 3.4 copy-start.3
  22.6 2.5 copy-start.4
  25.2 2.7 copy-start.10
  40.5 1.4 copy-start
  41.9 434.2 %all-reduce.5.cloned.1.call-start = ((), (), s32[]{:S(2)}) async-start(), calls=%async_computation.1 | async-start | bytes 2097152 | tf_op jit(solution)/shard_map/psum | solution.py:72
  52.6 1.0 copy-start.1
  53.7 154.1 %copy-start.8 = (bf16[16,128,512]{2,1,0:T(8,128)(2,1)S(1)}, bf16[16,128,512]{2,1,0:T(8,128)(2,1)}, u32[]{:S(2)}) copy-start(bf16[16,128,512]{2,1,0:T(8,128)(2,1)} %copy-done.7) | copy-start | bytes 6291460
  190.1 17.7 %copy-start.12 = (bf16[16,128,128]{2,1,0:T(8,128)(2,1)S(1)}, bf16[16,128,128]{2,1,0:T(8,128)(2,1)}, u32[]{:S(2)}) copy-start(bf16[16,128,128]{2,1,0:T(8,128)(2,1)} %copy-done.11) | copy-start | bytes 1572868
  193.1 285.2 %collective-permute-start = (bf16[1024,512]{1,0:T(8,128)(2,1)}, bf16[1024,512]{1,0:T(8,128)(2,1)}, u32[]{:S(2)}, u32[]{:S(2)}) collective-permute-start(bf16[1024,512]{1,0:T(8,128)(2,1)} %fusion.2), channel_id=1, source_target_pairs={{496,0},{0,16},{16,32},{32,48},{48,64},{64,80},{80,96},{96,112},{1... | collective-permute-start | bytes 3145736 | tf_op jit(solution)/shard_map/ppermute | solution.py:12
  210.5 6.2 %copy-start.5 = (bf16[512,512]{1,0:T(8,128)(2,1)S(1)}, bf16[512,512]{1,0:T(8,128)(2,1)}, u32[]{:S(2)}) copy-start(bf16[512,512]{1,0:T(8,128)(2,1)} %param.8) | copy-start | bytes 1572868
  216.7 259.3 %copy-start.6 = (bf16[512,512]{1,0:T(8,128)(2,1)S(1)}, bf16[512,512]{1,0:T(8,128)(2,1)}, u32[]{:S(2)}) copy-start(bf16[512,512]{1,0:T(8,128)(2,1)} %param.10) | copy-start | bytes 1572868
Sparse Core Ops, SparseCore 0:
  42.0 148.0 all-reduce.2
  193.0 283.0 all-reduce.4
where the time goes:
time: 488 us; the launch traced here: 487 us
  waiting for transfers between devices  395 us (81%)
  other arithmetic  31.6 us (6%)
  matrix products  18.2 us (4%)
  between operations  15 us (3%)
  starting transfers between devices  14.8 us (3%)
  local copies, waits for them, and re-layouts  13.1 us (3%)
    psum x1, waiting for transfers between devices, on_device(): tag_total = lax.psum(tag_grad, 'rot')  258 us
    psum x1, waiting for transfers between devices, on_device(): total = lax.psum(item_grad, 'tag')  136 us
    scatter-add x3, other arithmetic, spread_tiles(): return empty.at[index].add(tiles)  18.4 us
    ppermute x1, starting transfers between devices, shifted(): return lax.ppermute(block, axis, route)  14.7 us
  transfers between devices with their start and end apart: 3, of which 2 were waited for; matrix products, arithmetic and copies ran while one was open for 5% of the time, Pallas kernels for 0%

commit v1 on v0

--- a/solution.py
+++ b/solution.py
@@ -69,7 +69,8 @@
     items32 = item_factors.astype(jnp.float32)
     new_items = (items32 - 0.04 * (total + 0.05 * items32)).astype(jnp.bfloat16)
     rotated_items = shifted(new_items, "rot", 1)
-    tag_total = lax.psum(tag_grad, "rot")
+    opened = jax.lax.all_gather(tag_grad, "rot")
+    tag_total = jnp.sum(opened, axis=0)
     tags32 = tag_factors.astype(jnp.float32)
     new_tags = (tags32 - 0.04 * (tag_total + 0.05 * tags32)).astype(jnp.bfloat16)
     return (new_users, rotated_items, new_tags)

time: 488 us -> 336 us (0.69)
  waiting for transfers between devices: 395 us -> 228 us
  other arithmetic: 31.6 us -> 42.7 us
    psum x1 -> x0, waiting for transfers between devices: 258 us -> none  [on_device(): tag_total = lax.psum(tag_grad, 'rot')]
    psum x1, waiting for transfers between devices: 136 us -> 226 us  [on_device(): total = lax.psum(item_grad, 'tag')]
    reduce_sum x0 -> x1, other arithmetic: none -> 12.3 us  [on_device(): tag_total = jnp.sum(opened, axis=0)]
  transfers between devices with their start and end apart: 3 -> 3, of which waited for: 2 -> 2; matrix products, arithmetic and copies ran while one was open for 5% -> 7% of each run, Pallas kernels for 0% -> 0%
where the time goes in v1:
time: 336 us; the launch traced here: 334 us
  waiting for transfers between devices  228 us (68%)
  other arithmetic  42.7 us (13%)
  matrix products  18.3 us (5%)
  between operations  16.4 us (5%)
  starting transfers between devices  15.9 us (5%)
  local copies, waits for them, and re-layouts  13 us (4%)
    psum x1, waiting for transfers between devices, on_device(): total = lax.psum(item_grad, 'tag')  226 us
    scatter-add x3, other arithmetic, spread_tiles(): return empty.at[index].add(tiles)  18.4 us
    ppermute x1, starting transfers between devices, shifted(): return lax.ppermute(block, axis, route)  15.8 us
    reduce_sum x1, other arithmetic, on_device(): tag_total = jnp.sum(opened, axis=0)  12.3 us
  transfers between devices with their start and end apart: 3, of which 2 were waited for; matrix products, arithmetic and copies ran while one was open for 7% of the time, Pallas kernels for 0%

profile of v1, /device:TPU:1, one launch (start us, length us, event | category | flops | bytes accessed | tf_op | source)
XLA Modules:
  0.0 334.3 jit_solution(14610351181636947706)
XLA Ops:
  8.0 0.0 all-reduce.2.cloned.1.call-start
  8.0 0.8 fusion.13
  9.5 0.0 copy-start.2
  9.5 3.2 gather_fusion
  12.7 0.0 copy-done.2
  12.7 0.7 gather_fusion.1
  13.3 0.0 copy-start.7
  13.4 0.0 copy-start.9
  13.4 3.2 fusion.4
  16.5 0.0 copy-done.7
  16.6 0.0 copy-done.9
  16.6 0.0 copy-start.11
  16.6 0.0 copy-start.13
  16.6 2.7 fusion.17
  19.3 0.0 copy-done.11
  19.3 0.7 gather_fusion.2
  20.0 3.4 %gather_fusion.3 = bf16[16,128,512]{2,1,0:T(8,128)(2,1)} fusion(bf16[4,128,512]{2,1,0:T(8,128)(2,1)} %bitcast.34, s32[1024]{0:T(1024)S(1)} %get-tuple-element.9), kind=kCustom, calls=%fused_computation.3 | custom fusion | bytes 4194368 | tf_op jit(solution)/shard_map/gather | solution.py:51
  23.4 2.5 fusion.5
  26.0 0.0 copy-start.10
  26.0 2.7 fusion.18
  28.7 0.0 copy-done.10
  28.7 0.2 broadcast_in_dim.16
  28.9 6.2 %scatter_fusion.1 = f32[8,128,512]{2,1,0:T(8,128)S(1)} fusion(f32[8,128,512]{2,1,0:T(8,128)S(1)} %broadcast_in_dim.16, s32[16]{0:T(128)S(1)} %get-tuple-element.5, f32[16,128,512]{2,1,0:T(8,128)} %fusion.17), kind=kCustom, calls=%fused_computation.5 | custom fusion | flops 1048576 | bytes 12582976 | tf_op jit(solution)/shard_map/scatter-add | solution.py:17
  35.1 6.2 %scatter_fusion.2 = f32[8,128,512]{2,1,0:T(8,128)S(1)} fusion(f32[8,128,512]{2,1,0:T(8,128)S(1)} %scatter_fusion.1, s32[16]{0:T(128)S(1)} %get-tuple-element.4, f32[16,128,512]{2,1,0:T(8,128)} %fusion.18), kind=kCustom, calls=%fused_computation.6 | custom fusion | flops 1048576 | bytes 12582976 | tf_op jit(solution)/shard_map/scatter-add | solution.py:64
  41.3 1.3 copy-done
  42.6 0.0 all-reduce.2.cloned.1.call-update
  42.7 0.0 all-gather.2.cloned.1.call-start
  42.7 4.5 %fusion.19 = f32[16,128,512]{2,1,0:T(8,128)} fusion(bf16[16,128,128]{2,1,0:T(8,128)(2,1)} %copy-done.10, bf16[16,128,512]{2,1,0:T(8,128)(2,1)} %copy-done.3), kind=kOutput, calls=%fused_computation.44 | convolution fusion | flops 268435456 | bytes 6815744 | tf_op jit(solution)/shard_map/sij,sir->sjr/dot_general | solution.py:59
  47.2 0.1 broadcast.30.clone.1
  47.3 6.1 %scatter_fusion.3 = f32[4,128,512]{2,1,0:T(8,128)S(1)} fusion(f32[4,128,512]{2,1,0:T(8,128)S(1)} %broadcast.30.clone.1, s32[16]{0:T(128)S(1)} %get-tuple-element.3, f32[16,128,512]{2,1,0:T(8,128)} %fusion.19), kind=kCustom, calls=%fused_computation.7 | custom fusion | flops 1048576 | bytes 12582976 | tf_op jit(solution)/shard_map/scatter-add | solution.py:17
  53.4 1.0 copy-done.1
  54.4 0.0 all-gather.2.cloned.1.call-update
  54.4 0.0 copy-start.8
  54.4 226.0 %all-reduce.2.cloned.1.call-done = f32[1024,512]{1,0:T(8,128)} async-done(((f32[1024,512]{1,0:T(8,128)}), f32[1024,512]{1,0:T(8,128)}) %all-reduce.2.cloned.1.call-update) | async-done | bytes 2097168 | tf_op jit(solution)/shard_map/psum | solution.py:68
  280.5 3.0 fusion.2
  283.5 15.8 %collective-permute-start = (bf16[1024,512]{1,0:T(8,128)(2,1)}, bf16[1024,512]{1,0:T(8,128)(2,1)}, u32[]{:S(2)}, u32[]{:S(2)}) collective-permute-start(bf16[1024,512]{1,0:T(8,128)(2,1)} %fusion.2), channel_id=1, source_target_pairs={{496,0},{0,16},{16,32},{32,48},{48,64},{64,80},{80,96},{96,112},{1... | collective-permute-start | bytes 3145736 | tf_op jit(solution)/shard_map/ppermute | solution.py:12
  299.3 0.0 copy-done.8
  299.3 0.0 copy-done.12
  299.3 2.8 fusion.16
  302.1 0.1 broadcast.30.clone
  302.2 0.0 copy-start.5
  302.2 6.1 %scatter_fusion = f32[4,128,512]{2,1,0:T(8,128)S(1)} fusion(f32[4,128,512]{2,1,0:T(8,128)S(1)} %broadcast.30.clone, s32[16]{0:T(128)S(1)} %get-tuple-element.6, f32[16,128,512]{2,1,0:T(8,128)} %fusion.16), kind=kCustom, calls=%fused_computation.4 | custom fusion | flops 1048576 | bytes 12582976 | tf_op jit(solution)/shard_map/scatter-add | solution.py:17
  308.4 0.0 copy-done.5
  308.4 1.0 fusion.8
  309.4 2.0 collective-permute-done
  311.4 12.3 %reduce_sum.9 = f32[512,512]{1,0:T(8,128)S(1)} reduce(f32[32,512,512]{2,1,0:T(8,128)} %all-gather.2.cloned.1.call-done, f32[]{:T(128)} %constant.6.clone.1), dimensions={0}, to_apply=%region_5.6 | reduce | flops 8126464 | bytes 34603012 | tf_op jit(solution)/shard_map/reduce_sum | solution.py:73
  323.6 1.0 fusion.11
  324.6 2.3 copy.25
  (15 shorter events, 0.0 us)
Async XLA Ops:
  8.0 272.5 %all-reduce.2.cloned.1.call-start = ((), (), s32[]{:S(2)}) async-start(), calls=%async_computation | async-start | bytes 4194304 | tf_op jit(solution)/shard_map/psum | solution.py:68
  9.5 3.2 copy-start.2
  13.3 3.2 copy-start.7
  13.4 3.2 copy-start.9
  16.6 2.7 copy-start.11
  16.6 2.7 copy-start.13
  20.0 3.4 %copy-start.3 = (bf16[16,128,512]{2,1,0:T(8,128)(2,1)}, bf16[16,128,512]{2,1,0:T(8,128)(2,1)S(1)}, u32[]{:S(2)}) copy-start(bf16[16,128,512]{2,1,0:T(8,128)(2,1)S(1)} %gather_fusion.2) | copy-start | bytes 6291460
  23.4 2.5 copy-start.4
  26.0 2.7 copy-start.10
  41.3 1.3 copy-start
  42.7 268.7 %all-gather.2.cloned.1.call-start = ((), (), s32[]{:S(2)}) async-start(), calls=%async_computation.1 | async-start | bytes 34603008 | tf_op jit(solution)/shard_map/all_gather | solution.py:72
  53.4 1.0 copy-start.1
  54.4 244.9 %copy-start.8 = (bf16[16,128,512]{2,1,0:T(8,128)(2,1)S(1)}, bf16[16,128,512]{2,1,0:T(8,128)(2,1)}, u32[]{:S(2)}) copy-start(bf16[16,128,512]{2,1,0:T(8,128)(2,1)} %copy-done.7) | copy-start | bytes 6291460
  280.5 18.9 %copy-start.12 = (bf16[16,128,128]{2,1,0:T(8,128)(2,1)S(1)}, bf16[16,128,128]{2,1,0:T(8,128)(2,1)}, u32[]{:S(2)}) copy-start(bf16[16,128,128]{2,1,0:T(8,128)(2,1)} %copy-done.11) | copy-start | bytes 1572868
  283.5 27.9 %collective-permute-start = (bf16[1024,512]{1,0:T(8,128)(2,1)}, bf16[1024,512]{1,0:T(8,128)(2,1)}, u32[]{:S(2)}, u32[]{:S(2)}) collective-permute-start(bf16[1024,512]{1,0:T(8,128)(2,1)} %fusion.2), channel_id=1, source_target_pairs={{496,0},{0,16},{16,32},{32,48},{48,64},{64,80},{80,96},{96,112},{1... | collective-permute-start | bytes 3145736 | tf_op jit(solution)/shard_map/ppermute | solution.py:12
  302.2 6.1 %copy-start.5 = (bf16[512,512]{1,0:T(8,128)(2,1)S(1)}, bf16[512,512]{1,0:T(8,128)(2,1)}, u32[]{:S(2)}) copy-start(bf16[512,512]{1,0:T(8,128)(2,1)} %param.8) | copy-start | bytes 1572868
  309.4 14.3 %copy-start.6 = (bf16[512,512]{1,0:T(8,128)(2,1)S(1)}, bf16[512,512]{1,0:T(8,128)(2,1)}, u32[]{:S(2)}) copy-start(bf16[512,512]{1,0:T(8,128)(2,1)} %param.10) | copy-start | bytes 1572868
Sparse Core Ops, SparseCore 0:
  42.8 237.6 all-reduce.1
Sparse Core Ops, SparseCore 1:
  54.5 242.7 all-gather.1
